TPU v7x, 256 devices: a whole 4x4x8 slice. The times are simulated.
256 devices in a mesh: seq: 32 (over y, z), tp: 8 (over x, core).
Axes of the slice: x: 4, y: 4, z: 8, core: 2. Of those that a mesh axis runs over, the one named last changes fastest.
Arguments:
- values_in: bfloat16 [16384, 8192], P('seq', 'tp'), may hold values from -6 to 6
- gates_in: bfloat16 [16384, 8192], P('seq', 'tp'), may hold values from -6 to 6
- keys_in: bfloat16 [16384, 1024], P('seq', 'tp'), may hold values from -6 to 6
- queries_in: bfloat16 [16384, 1024], P('seq', 'tp'), may hold values from -6 to 6
- log_decay: float32 [128, 16384], P('tp', 'seq'), may hold values from -2 to 0, as said below
- conv_values: float32 [4, 8192], P(None, 'tp'), may hold values from -3 to 3
- bias_values: float32 [8192], P('tp'), may hold values from -3 to 3
- conv_keys: float32 [4, 1024], P(None, 'tp'), may hold values from -3 to 3
- bias_keys: float32 [1024], P('tp'), may hold values from -3 to 3
- conv_queries: float32 [4, 1024], P(None, 'tp'), may hold values from -3 to 3
- bias_queries: float32 [1024], P('tp'), may hold values from -3 to 3
- skip_scale: float32 [128], P('tp'), may hold values from 0.5 to 1.5
- norm_gain: float32 [8192], P('tp'), may hold values from 0.1 to 1.9
- out_weight: bfloat16 [8192, 4096], P('tp'), may hold values from -0.09375 to 0.09375
Outputs:
- mixer_out: bfloat16 [16384, 4096], P('seq', 'tp')
Inputs may be any that keep to these rules, and one draw needn't show every extreme that they name: `log_decay`: every entry is below zero.
All inputs are finite; a program needn't handle non-finite values.
Results may differ from a plain program's by a relative error of at most 0.015.
Values may be sent and summed in bfloat16 or wider, within the bound.
A program may use at most 64 MiB of HBM per device.

v0:
```python
from functools import partial

import jax
import jax.numpy as jnp
from jax import lax
from jax.sharding import PartitionSpec as P

N = 128


HIGH = lax.Precision.HIGHEST
norm_epsilon = 1e-05


def passed_along(block, axis, distance):
    devices = range(lax.axis_size(axis))
    route = [(i - distance, i) for i in devices if i - distance in devices]
    return lax.ppermute(block, axis, route)


def causal_filter(padded, kernel_weights, conv_bias, row_total):
    width = kernel_weights.shape[0]
    running = jnp.broadcast_to(conv_bias[None, :], (row_total, conv_bias.shape[0]))
    for offset in range(width):
        running = running + kernel_weights[offset][None, :] * padded[
            offset : offset + row_total
        ].astype(jnp.float32)
    return jax.nn.silu(running).astype(jnp.bfloat16)


def block_terms(carried, inputs, per_group):
    values, keys_block, queries, logs = inputs
    row_total = values.shape[0]
    groups = keys_block.shape[1]
    cumulative = jnp.cumsum(logs, axis=1)
    scores = jnp.einsum("tgn,sgn->gts", queries, keys_block, preferred_element_type=jnp.float32)
    positions = lax.broadcasted_iota(jnp.int32, (row_total, row_total), 0)
    sources = lax.broadcasted_iota(jnp.int32, (row_total, row_total), 1)
    log_gaps = jnp.where(
        (positions >= sources)[None], cumulative[:, :, None] - cumulative[:, None, :], -jnp.inf
    )
    mixing = (
        jnp.exp(log_gaps).reshape(groups, per_group, row_total, row_total) * scores[:, None]
    ).astype(jnp.bfloat16)
    local_part = jnp.einsum("ghts,sghp->tghp", mixing, values, preferred_element_type=jnp.float32)
    growth = jnp.exp(cumulative).T.reshape(row_total, groups, per_group, 1)
    from_state = (
        jnp.einsum("tgn,ghnp->tghp", queries.astype(jnp.float32), carried, precision=HIGH) * growth
    )
    remaining = jnp.exp(cumulative[:, -1:] - cumulative).T.reshape(row_total, groups, per_group, 1)
    weighted_keys = keys_block.astype(jnp.float32)[:, :, None, :] * remaining
    fresh_state = jnp.einsum(
        "tghn,tghp->ghnp", weighted_keys, values.astype(jnp.float32), precision=HIGH
    )
    carried = jnp.exp(cumulative[:, -1]).reshape(groups, per_group, 1, 1) * carried + fresh_state
    return (carried, local_part + from_state)


def shards(
    values_in,
    gates_in,
    keys_in,
    queries_in,
    log_decay,
    conv_values,
    bias_values,
    conv_keys,
    bias_keys,
    conv_queries,
    bias_queries,
    skip_scale,
    norm_gain,
    out_weight,
):
    row_total = values_in.shape[0]
    head_count = log_decay.shape[0]
    inner_width = values_in.shape[1]
    head_size = inner_width // head_count
    key_width = keys_in.shape[1]
    groups = key_width // N
    per_group = head_count // groups
    margin = conv_values.shape[0] - 1
    rim_send = jnp.concatenate(
        [
            values_in[row_total - margin :],
            keys_in[row_total - margin :],
            queries_in[row_total - margin :],
        ],
        axis=1,
    )
    rim_rows = passed_along(rim_send, "seq", 1)
    values = causal_filter(
        jnp.concatenate([rim_rows[:, :inner_width], values_in], axis=0),
        conv_values,
        bias_values,
        row_total,
    )
    keys_all = causal_filter(
        jnp.concatenate([rim_rows[:, inner_width : inner_width + key_width], keys_in], axis=0),
        conv_keys,
        bias_keys,
        row_total,
    )
    queries_all = causal_filter(
        jnp.concatenate([rim_rows[:, inner_width + key_width :], queries_in], axis=0),
        conv_queries,
        bias_queries,
        row_total,
    )
    block_rows = min(row_total, 512)
    block_count = row_total // block_rows
    value_blocks = values.reshape(block_count, block_rows, groups, per_group, head_size)
    key_blocks = keys_all.reshape(block_count, block_rows, groups, N)
    query_blocks = queries_all.reshape(block_count, block_rows, groups, N)
    log_blocks = log_decay.reshape(head_count, block_count, block_rows).transpose(1, 0, 2)
    initial = jnp.zeros((groups, per_group, N, head_size), jnp.float32)
    local_end, outputs = lax.scan(
        partial(block_terms, per_group=per_group),
        initial,
        (value_blocks, key_blocks, query_blocks, log_blocks),
    )
    cumulative = jnp.cumsum(log_decay, axis=1)
    device_log = cumulative[:, -1]
    flat_end = local_end.reshape(head_count, N * head_size)
    all_logs = lax.all_gather(device_log[None, :], "seq", axis=0, tiled=True)
    inclusive = jnp.cumsum(all_logs, axis=0)
    own_index = lax.axis_index("seq")
    before_mine = lax.dynamic_index_in_dim(inclusive - all_logs, own_index, 0, keepdims=False)
    pieces = lax.all_gather(flat_end[None].astype(jnp.bfloat16), "seq", axis=0, tiled=True).astype(
        jnp.float32
    )
    shard_ids = jnp.arange(pieces.shape[0], dtype=jnp.int32)
    through_shard = jnp.take(inclusive, shard_ids, axis=0)
    exponent = jnp.where(
        (shard_ids < own_index)[:, None], before_mine[None, :] - through_shard, -jnp.inf
    )
    incoming = jnp.zeros_like(flat_end) + jnp.einsum(
        "kh,khm->hm", jnp.exp(exponent), pieces, precision=HIGH
    )
    incoming = incoming.reshape(groups, per_group, N, head_size)
    growth = jnp.exp(cumulative).T.reshape(row_total, groups, per_group, 1)
    query_rows = queries_all.reshape(row_total, groups, N).astype(jnp.float32)
    from_before = jnp.einsum("tgn,ghnp->tghp", query_rows, incoming, precision=HIGH) * growth
    mixed = outputs.reshape(row_total, groups, per_group, head_size) + from_before
    mixed = mixed + skip_scale.reshape(groups, per_group)[None, :, :, None] * values.reshape(
        row_total, groups, per_group, head_size
    ).astype(jnp.float32)
    gated_rows = mixed.reshape(row_total, groups, per_group * head_size) * jax.nn.silu(
        gates_in.reshape(row_total, groups, per_group * head_size).astype(jnp.float32)
    )
    mean_square = jnp.mean(gated_rows * gated_rows, axis=-1, keepdims=True)
    normed = (
        (
            gated_rows
            * lax.rsqrt(mean_square + norm_epsilon)
            * norm_gain.reshape(groups, per_group * head_size)
        )
        .astype(jnp.bfloat16)
        .reshape(row_total, inner_width)
    )
    local_sum = jnp.dot(normed, out_weight, preferred_element_type=jnp.float32)
    summed = lax.psum(local_sum.astype(jnp.bfloat16), "tp").astype(jnp.float32)
    column_width = summed.shape[1] // lax.axis_size("tp")
    result = lax.dynamic_slice_in_dim(summed, lax.axis_index("tp") * column_width, column_width, 1)
    return result.astype(jnp.bfloat16)


def solution(mesh):
    placed = (
        P("seq", "tp"),
        P("seq", "tp"),
        P("seq", "tp"),
        P("seq", "tp"),
        P("tp", "seq"),
        P(None, "tp"),
        P("tp"),
        P(None, "tp"),
        P("tp"),
        P(None, "tp"),
        P("tp"),
        P("tp"),
        P("tp"),
        P("tp", None),
    )
    return jax.shard_map(
        shards, mesh=mesh, in_specs=placed, out_specs=P("seq", "tp"), check_vma=False
    )
```

profile of v0, /device:TPU:1, one launch (start us, length us, event | category | flops | bytes accessed | tf_op | source)
XLA Modules:
  0.0 247.5 jit_solution(196115072066289706)
XLA Ops:
  6.5 0.0 copy-start
  6.5 0.0 all-gather.3.cloned.1.call-start
  6.6 0.8 slice.96
  7.4 0.7 slice.97
  8.1 0.7 slice.98
  8.8 0.3 copy.48
  9.0 4.4 %collective-permute-start = (bf16[3,1280]{0,1:T(8,128)(2,1)S(1)}, bf16[3,1280]{0,1:T(8,128)(2,1)S(1)}, u32[]{:S(2)}, u32[]{:S(2)}) collective-permute-start(bf16[3,1280]{0,1:T(8,128)(2,1)S(1)} %copy.48), channel_id=1, source_target_pairs={{0,8},{8,16},{16,24},{24,32},{32,40},{40,48},{48,56},{56,64},{64,7... | collective-permute-start | bytes 23048 | tf_op jit(solution)/shard_map/ppermute | solution.py:18
  13.4 0.0 copy-done
  13.4 1.2 reduce-window.12
  14.6 0.2 slice_reduce_fusion
  14.8 0.1 copy_bitcast_fusion.1
  14.8 0.2 slice_reduce_fusion.1
  15.0 0.9 fusion.41
  15.9 0.8 slice_bitcast_fusion.3
  16.8 0.1 exponential_bitcast_fusion.1
  16.9 1.5 copy.49
  18.4 1.4 collective-permute-done
  19.8 0.1 copy.54
  19.8 0.0 copy-done.5
  19.8 0.0 copy-done.9
  19.9 0.2 fusion.39
  20.1 0.0 copy-done.7
  20.1 2.7 %multiply_convert_fusion.3 = bf16[512,1024]{0,1:T(8,128)(2,1)S(1)} fusion(bf16[512,1024]{0,1:T(8,128)(2,1)S(1)} %copy.49, bf16[3,1024]{0,1:T(8,128)(2,1)S(1)} %slice.127, f32[1024]{0:T(1024)S(1)} %bitcast.91, f32[1024]{0:T(1024)S(1)} %bitcast.92, f32[1024]{0:T(1024)S(1)} %bitcast.90, f32[1024]{0:T(1024)S(1)} %bitcast.89, f32[1024]{0:T(1024)S(1)} %copy-done.7), kind=kLoop, calls=%fused_computation.25 | loop fusion | flops 13631488 | bytes 2123776 | tf_op jit(solution)/shard_map/convert_element_type | solution.py:28
  22.8 0.0 copy-start.13
  22.8 0.0 copy-start.3
  22.8 2.4 fusion.18
  25.2 0.0 copy-start.8
  25.2 0.0 copy-start.6
  25.2 0.0 copy-start.10
  25.2 0.3 copy.55
  25.5 1.2 convert_element_type.126
  26.7 0.0 all-gather.3.cloned.1.call-update
  26.7 0.0 all-reduce.3.cloned.1.call-start
  26.8 0.0 copy-done.13
  26.8 0.6 dynamic-slice.1
  28.1 0.2 dynamic-update-slice
  28.3 65.2 %all-reduce = f32[512]{0:T(512)S(1)} all-reduce(f32[512]{0:T(512)S(1)} %dynamic-update-slice), channel_id=2, replica_groups=mesh['seq'=32,'tp'=8] {'seq'}, use_global_device_ids=true, to_apply=%add | all-reduce | flops 512 | bytes 4096
  93.5 0.1 reshape.221
  93.6 0.1 reduce_window_sum.40
  93.6 0.6 gather_fusion
  94.3 0.1 exponential_bitcast_fusion.2
  94.3 0.1 copy.58
  94.4 0.0 copy-done.3
  94.4 1.3 copy.57
  95.7 0.8 iota_compare_fusion
  96.6 0.1 copy.53
  96.6 0.0 copy-done.10
  96.7 0.2 multiply_convert_fusion.6
  96.9 0.3 fusion.42
  97.1 1.0 fusion.25
  98.1 5.8 %fusion.2 = f32[16,64,512]{2,1,0:T(8,128)} fusion(bf16[512,16,64]{0,2,1:T(8,128)(2,1)S(1)} %bitcast.86, f32[512,512]{1,0:T(8,128)S(1)} %fusion.42, f32[16,512]{1,0:T(8,128)S(1)} %copy_bitcast_fusion.1, pred[512,512]{1,0:T(8,128)(4,1)S(1)} %copy-done.4), kind=kOutput, calls=%fused_computation.4 | convolution fusion | flops 553648128 | bytes 4489216 | tf_op jit(solution)/shard_map/while/body/eval_jaxpr/ghts,sghp->tghp/dot_general | solution.py:45
  104.0 25.7 %all-gather.3.cloned.1.call-done = bf16[32,16,8192]{2,1,0:T(8,128)(2,1)} async-done(((bf16[1,16,8192]{2,1,0:T(8,128)(2,1)}), bf16[32,16,8192]{2,1,0:T(8,128)(2,1)}) %all-gather.3.cloned.1.call-update) | async-done | bytes 8388624 | tf_op jit(solution)/shard_map/all_gather | solution.py:129
  129.7 16.9 %fusion = f32[16,1,8192]{2,1,0:T(1,128)S(1)} fusion(f32[32,16,1]{0,2,1:T(1,128)S(1)} %copy.58, bf16[32,16,8192]{2,1,0:T(8,128)(2,1)} %all-gather.3.cloned.1.call-done), kind=kOutput, calls=%fused_computation.2 | convolution fusion | flops 50331648 | bytes 8914944 | tf_op jit(solution)/shard_map/kh,khm->hm/dot_general | solution.py:137
  146.5 1.1 copy.73
  147.6 2.5 reshape.210
  150.1 3.2 %fusion.31 = f32[16,64,512]{2,1,0:T(8,128)S(1)} fusion(f32[16,128,64]{2,1,0:T(8,128)} %reshape.210, bf16[512,128]{1,0:T(8,128)(2,1)S(1)} %multiply_convert_fusion.6), kind=kOutput, calls=%fused_computation.54 | convolution fusion | flops 805306368 | bytes 2752512 | tf_op jit(solution)/shard_map/tgn,ghnp->tghp/dot_general | solution.py:143
  153.3 0.0 copy-done.11
  153.4 1.0 fusion.10
  154.3 0.2 copy-done.1
  154.6 0.7 multiply_reduce_fusion
  155.3 9.7 %convolution_convert_fusion = bf16[512,4096]{1,0:T(8,128)(2,1)} fusion(bf16[1024,4096]{1,0:T(8,128)(2,1)} %param.27, f32[512,1024]{0,1:T(8,128)S(1)} %get-tuple-element.18, f32[1024]{0:T(1024)S(1)} %copy-done.12, f32[512]{0:T(512)S(1)} %add_rsqrt_fusion), kind=kOutput, calls=%fused_computation.6 | convolution fusion | flops 4298637312 | bytes 14686208 | tf_op jit(solution)/shard_map/dot_general | solution.py:161
  165.0 0.0 all-reduce.3.cloned.1.call-update
  165.0 73.7 %all-reduce.3.cloned.1.call-done = bf16[512,4096]{1,0:T(8,128)(2,1)} async-done(((bf16[512,4096]{1,0:T(8,128)(2,1)}), bf16[512,4096]{1,0:T(8,128)(2,1)}) %all-reduce.3.cloned.1.call-update) | async-done | bytes 4194320 | tf_op jit(solution)/shard_map/psum | solution.py:162
  238.8 1.9 convert_convert_fusion
  (27 shorter events, 0.1 us)
Async XLA Ops:
  6.5 6.9 %copy-start = (f32[16,512]{1,0:T(8,128)S(1)}, f32[16,512]{1,0:T(8,128)}, u32[]{:S(2)}) copy-start(f32[16,512]{1,0:T(8,128)} %param.18) | copy-start | bytes 98308
  6.5 13.3 %copy-start.5 = (bf16[512,128]{1,0:T(8,128)(2,1)S(1)}, bf16[512,128]{1,0:T(8,128)(2,1)}, u32[]{:S(2)}) copy-start(bf16[512,128]{1,0:T(8,128)(2,1)} %param.16) | copy-start | bytes 393220
  6.5 13.3 %copy-start.9 = (f32[128]{0:T(128)S(1)}, f32[128]{0:T(128)}, u32[]{:S(2)}) copy-start(f32[128]{0:T(128)} %param.22) | copy-start | bytes 1540
  6.5 13.6 %copy-start.7 = (f32[1024]{0:T(1024)S(1)}, f32[1024]{0:T(1024)}, u32[]{:S(2)}) copy-start(f32[1024]{0:T(1024)} %param.20) | copy-start | bytes 12292
  6.5 123.1 %all-gather.3.cloned.1.call-start = ((), (), s32[]{:S(2)}) async-start(), calls=%async_computation | async-start | bytes 8650752 | tf_op jit(solution)/shard_map/all_gather | solution.py:129
  9.0 10.7 %collective-permute-start = (bf16[3,1280]{0,1:T(8,128)(2,1)S(1)}, bf16[3,1280]{0,1:T(8,128)(2,1)S(1)}, u32[]{:S(2)}, u32[]{:S(2)}) collective-permute-start(bf16[3,1280]{0,1:T(8,128)(2,1)S(1)} %copy.48), channel_id=1, source_target_pairs={{0,8},{8,16},{16,24},{24,32},{32,40},{40,48},{48,56},{56,64},{64,7... | collective-permute-start | bytes 23048 | tf_op jit(solution)/shard_map/ppermute | solution.py:18
  22.8 4.0 %copy-start.13 = (u32[256]{0:T(256)S(1)}, u32[256]{0:T(256)}, u32[]{:S(2)}) copy-start(u32[256]{0:T(256)} %constant.80) | copy-start | bytes 3076
  22.8 71.6 %copy-start.3 = (bf16[512,1024]{1,0:T(8,128)(2,1)S(1)}, bf16[512,1024]{1,0:T(8,128)(2,1)}, u32[]{:S(2)}) copy-start(bf16[512,1024]{1,0:T(8,128)(2,1)} %param.15) | copy-start | bytes 3145732
  25.2 71.3 %copy-start.8 = (f32[4,128]{1,0:T(4,128)S(1)}, f32[4,128]{1,0:T(4,128)}, u32[]{:S(2)}) copy-start(f32[4,128]{1,0:T(4,128)} %param.23) | copy-start | bytes 6148
  25.2 71.4 %copy-start.6 = (bf16[512,128]{1,0:T(8,128)(2,1)S(1)}, bf16[512,128]{1,0:T(8,128)(2,1)}, u32[]{:S(2)}) copy-start(bf16[512,128]{1,0:T(8,128)(2,1)} %param.17) | copy-start | bytes 393220
  25.2 71.4 %copy-start.10 = (f32[128]{0:T(128)S(1)}, f32[128]{0:T(128)}, u32[]{:S(2)}) copy-start(f32[128]{0:T(128)} %param.24) | copy-start | bytes 1540
  26.7 212.0 %all-reduce.3.cloned.1.call-start = ((), (), s32[]{:S(2)}) async-start(), calls=%async_computation.1 | async-start | bytes 8388608 | tf_op jit(solution)/shard_map/psum | solution.py:162
  96.6 1.5 copy-start.4
  147.6 5.7 %copy-start.11 = (f32[16]{0:T(128)S(1)}, f32[16]{0:T(128)}, u32[]{:S(2)}) copy-start(f32[16]{0:T(128)} %param.25) | copy-start | bytes 196
  150.1 3.2 %copy-start.2 = (f32[16,64,512]{2,1,0:T(8,128)S(1)}, f32[16,64,512]{2,1,0:T(8,128)}, u32[]{:S(2)}) copy-start(f32[16,64,512]{2,1,0:T(8,128)} %fusion.2) | copy-start | bytes 6291460
  153.3 1.2 copy-start.1
  154.6 0.7 copy-start.12
Sparse Core Ops, SparseCore 0:
  26.9 102.7 all-gather.2
  165.1 73.5 all-reduce.2
where the time goes:
time: 249 us; the launch traced here: 247 us
  waiting for transfers between devices  101 us (41%)
  blocking collectives  65.2 us (26%)
  matrix products  39.3 us (16%)
  local copies, waits for them, and re-layouts  14.4 us (6%)
  between operations  14.3 us (6%)
  other arithmetic  8.96 us (4%)
  starting transfers between devices  4.45 us (2%)
    psum x1, waiting for transfers between devices, shards(): summed = lax.psum(local_sum.astype(jnp.bfloat16), 'tp').astype(jnp.float32)  73.7 us
    unnamed x1, blocking collectives  65.2 us
    all_gather x1, waiting for transfers between devices, shards(): lax.all_gather(flat_end[None].astype(jnp.bfloat16), 'seq', axis=0, tiled=...  25.7 us
    dot_general x1, matrix products, shards(): jnp.einsum('kh,khm->hm', jnp.exp(exponent), pieces, precision=HIGH)  16.9 us
    dot_general x1, matrix products, shards(): local_sum = jnp.dot(normed, out_weight, preferred_element_type=jnp.float32)  9.74 us
    dot_general x1, matrix products, block_terms(): jnp.einsum('ghts,sghp->tghp', mixing, values, preferred_element_type=jnp....  5.8 us
  transfers between devices with their start and end apart: 3, of which 3 were waited for; matrix products, arithmetic and copies ran while one was open for 7% of the time, Pallas kernels for 0%

commit v1 on v0

v1 whole, which is shorter than its diff:
```python
import functools

import jax
import jax.numpy as jnp
from jax import lax
from jax.experimental import pallas as pl
from jax.experimental.pallas import tpu as pltpu
from jax.sharding import PartitionSpec as P

MESH = pl.DeviceIdType.MESH
F32 = jnp.float32
BF16 = jnp.bfloat16
EPS = 1e-05
CH = 128
PAD = 16
LANES = 128


def dot(a, b):
    return jnp.dot(a, b, preferred_element_type=F32)


def silu(v):
    h = 0.5 * v
    return h + h * jnp.tanh(h)


def parts_of(x):
    hi = x.astype(BF16).astype(F32)
    rest = x - hi
    mid = rest.astype(BF16).astype(F32)
    return hi, mid, rest - mid


def kernel(
    n_seq,
    v_hbm,
    g_hbm,
    k_hbm,
    q_hbm,
    log_ref,
    cv_ref,
    bv_ref,
    ck_ref,
    bk_ref,
    cq_ref,
    bq_ref,
    skip_ref,
    gain_ref,
    w_hbm,
    out_ref,
    xpad,
    gates,
    wbuf,
    spread,
    ct,
    cs,
    grow,
    rem,
    ap,
    vals,
    vw,
    keys_t,
    qs,
    fresh,
    s_loc,
    mixed,
    abuf,
    ra,
    fbuf,
    rf,
    sbuf,
    s_in,
    y,
    p_send,
    p_recv,
    own,
    h_send,
    h_recv,
    d_send,
    d_recv,
    c_send,
    c_recv,
    in_sem,
    w_sem,
    halo_s,
    halo_r,
    a_s,
    a_r,
    f_s,
    f_r,
    s_s,
    s_r,
    p_s,
    p_r,
    h_s,
    h_r,
    d_s,
    d_r,
    c_s,
    c_r,
):
    rows, width = v_hbm.shape
    heads = log_ref.shape[0]
    chunks = rows // CH
    slabs = width // LANES
    split = n_seq // slabs
    seg = 128 // split
    half = rows // 2
    quarter = half // 2
    tp_size = lax.axis_size("tp")
    me = lax.axis_index("seq")
    tp = lax.axis_index("tp")
    core = lax.rem(tp, 2)
    mate = tp + 1 - 2 * core
    ahead = lax.rem(tp + 2, tp_size)
    behind = lax.rem(tp + tp_size - 2, tp_size)
    far = lax.rem(tp + 4, tp_size)

    barrier = pltpu.get_barrier_semaphore()

    def greet(i, _):
        pl.semaphore_signal(
            barrier, inc=1, device_id={"seq": lax.rem(me + i, n_seq)}, device_id_type=MESH
        )
        return 0

    lax.fori_loop(1, n_seq, greet, 0)
    for other in (mate, ahead, behind):
        pl.semaphore_signal(barrier, inc=1, device_id={"tp": other}, device_id_type=MESH)

    loads = [
        pltpu.make_async_copy(v_hbm, xpad.at[pl.ds(PAD, rows), pl.ds(0, width)], in_sem.at[0]),
        pltpu.make_async_copy(
            k_hbm, xpad.at[pl.ds(PAD, rows), pl.ds(width, 128)], in_sem.at[1]
        ),
        pltpu.make_async_copy(
            q_hbm, xpad.at[pl.ds(PAD, rows), pl.ds(width + 128, 128)], in_sem.at[2]
        ),
        pltpu.make_async_copy(g_hbm, gates, in_sem.at[3]),
    ]
    for load in loads:
        load.start()
    cols = w_hbm.shape[1] // tp_size
    w_loads = []
    for j in range(8):
        chip = (far, ahead, behind, tp)[j // 2]
        owner = chip - core + (1 - core if j % 2 == 0 else core)
        w_loads.append(
            pltpu.make_async_copy(
                w_hbm.at[:, pl.ds(pl.multiple_of(owner * cols, cols), cols)],
                wbuf.at[j],
                w_sem.at[j],
            )
        )
    for load in w_loads:
        load.start()

    lane_head = lax.broadcasted_iota(jnp.int32, (2 * heads, width), 1) // (width // heads)
    row_head = lax.broadcasted_iota(jnp.int32, (2 * heads, width), 0)
    row_head = jnp.where(row_head >= heads, row_head - heads, row_head)
    spread[...] = jnp.where(lane_head == row_head, 1.0, 0.0).astype(BF16)

    def expand(x):
        hi = x.astype(BF16).astype(F32)
        return jnp.concatenate([hi, x - hi], axis=1).astype(BF16)

    low_a = lax.broadcasted_iota(jnp.int32, (CH, CH), 0)
    low_b = lax.broadcasted_iota(jnp.int32, (CH, CH), 1)
    lower = jnp.where(low_b <= low_a, 1.0, 0.0)
    lower3 = jnp.concatenate([lower] * 3, axis=1).astype(BF16)
    upper = jnp.where(low_a <= low_b, 1.0, 0.0)
    upper3 = jnp.concatenate([upper] * 3, axis=0).astype(BF16)

    def decay(c, _):
        at = pl.ds(pl.multiple_of(c * CH, CH), CH)
        logs = jnp.concatenate(parts_of(log_ref[:, at]), axis=1).astype(BF16)
        col = lax.dot_general(lower3, logs, (((1,), (1,)), ((), ())), preferred_element_type=F32)
        ct[c] = col
        cs[c] = dot(logs, upper3)
        g2 = expand(jnp.exp(col))
        r2 = expand(jnp.exp(jnp.minimum(col[CH - 1 : CH, :] - col, 0.0)))
        for j in range(width // 256):
            sl = slice(j * 256, (j + 1) * 256)
            grow[at, sl] = dot(g2, spread[:, sl])
            rem[at, sl] = dot(r2, spread[:, sl])
        return 0

    lax.fori_loop(0, chunks, decay, 0)
    before = jnp.ones((1, width), F32)
    for c in range(chunks):
        ap[c] = jnp.broadcast_to(before, (8, width))
        before = before * grow[c * CH + CH - 1 : c * CH + CH, :]
    for q in range(slabs):
        abuf[q] = jnp.broadcast_to(before[:, q * LANES : (q + 1) * LANES], (8, LANES))
    skip8 = jnp.broadcast_to(skip_ref[...], (8, heads))

    pl.semaphore_wait(barrier, n_seq - 1 + 3)

    after = {"seq": lax.rem(me + 1, n_seq)}
    halos = []
    for i, (src, lo, wid) in enumerate(
        ((v_hbm, 0, width), (k_hbm, width, 128), (q_hbm, width + 128, 128))
    ):
        halos.append(
            pltpu.make_async_remote_copy(
                src_ref=src.at[pl.ds(rows - PAD, PAD), :],
                dst_ref=xpad.at[pl.ds(0, PAD), pl.ds(lo, wid)],
                send_sem=halo_s.at[i],
                recv_sem=halo_r.at[i],
                device_id=after,
                device_id_type=MESH,
            )
        )
    for halo in halos:
        halo.start()

    def a_copy(peer, slot):
        return pltpu.make_async_remote_copy(
            src_ref=abuf.at[peer // split],
            dst_ref=ra.at[slot],
            send_sem=a_s.at[peer],
            recv_sem=a_r.at[slot],
            device_id={"seq": peer},
            device_id_type=MESH,
        )

    def f_copy(peer, slot):
        return pltpu.make_async_remote_copy(
            src_ref=fbuf.at[peer],
            dst_ref=rf.at[slot],
            send_sem=f_s.at[peer],
            recv_sem=f_r.at[slot],
            device_id={"seq": peer},
            device_id_type=MESH,
        )

    def s_copy(peer, slot):
        return pltpu.make_async_remote_copy(
            src_ref=sbuf.at[peer],
            dst_ref=s_in.at[slot],
            send_sem=s_s.at[peer],
            recv_sem=s_r.at[slot],
            device_id={"seq": peer},
            device_id_type=MESH,
        )

    def send_a(i, _):
        a_copy(lax.rem(me + i, n_seq), me).start()
        return 0

    lax.fori_loop(1, n_seq, send_a, 0)
    ra[me] = abuf[me // split]

    def conv(c):
        at = pl.ds(pl.multiple_of(c * CH, CH), CH)
        window = pl.ds(pl.multiple_of(c * CH, CH), CH + PAD)

        def taps(lo, w_ref, b_ref, off):
            x = xpad[window, lo : lo + LANES].astype(F32)
            sl = slice(off, off + LANES)
            acc = b_ref[:, sl] + w_ref[3:4, sl] * x[PAD:]
            for back in range(1, 4):
                acc = acc + w_ref[3 - back : 4 - back, sl] * pltpu.roll(x, back, axis=0)[PAD:]
            return silu(acc).astype(BF16)

        keys = taps(width, ck_ref, bk_ref, 0)
        kt = keys.astype(F32).T.astype(BF16)
        keys_t[c] = kt
        qs[at, :] = taps(width + 128, cq_ref, bq_ref, 0)
        for j in range(slabs):
            sl = slice(j * LANES, (j + 1) * LANES)
            v = taps(j * LANES, cv_ref, bv_ref, j * LANES)
            vals[at, sl] = v
            vw[:, sl] = (v.astype(F32) * rem[at, sl]).astype(BF16)
        for j in range(width // 256):
            sl = slice(j * 256, (j + 1) * 256)
            fresh[c, :, sl] = dot(kt, vw[:, sl])

    for load in loads[:3]:
        load.wait()

    def conv_step(i, _):
        conv(chunks - i)
        return 0

    lax.fori_loop(1, chunks, conv_step, 0)
    for halo in halos:
        halo.wait_recv()

    @pl.when(me == 0)
    def _():
        xpad[0:PAD, :] = jnp.zeros((PAD, xpad.shape[1]), BF16)

    conv(0)

    for q in range(slabs):
        sl = slice(q * LANES, (q + 1) * LANES)
        s = fresh[0, :, sl]
        s_loc[0, :, sl] = jnp.zeros((128, LANES), BF16)
        for c in range(1, chunks):
            s_loc[c, :, sl] = s.astype(BF16)
            s = grow[c * CH + CH - 1 : c * CH + CH, sl] * s + fresh[c, :, sl]
        f = s.astype(BF16)
        for r in range(split):
            fbuf[q * split + r] = f[r * seg : (r + 1) * seg]

    def send_f(i, _):
        f_copy(lax.rem(me + i, n_seq), me).start()
        return 0

    lax.fori_loop(1, n_seq, send_f, 0)
    rf[me] = fbuf[me]

    skip_row = dot(expand(skip8), spread[...])
    lane = lax.broadcasted_iota(jnp.int32, (1, LANES), 1)
    first = jnp.where(lane < LANES // 2, 1.0, 0.0).astype(BF16)
    second = jnp.where(lane < LANES // 2, 0.0, 1.0).astype(BF16)

    def local(c, _):
        at = pl.ds(pl.multiple_of(c * CH, CH), CH)
        qc = qs[at, :]
        scores = jnp.where(low_b <= low_a, dot(qc, keys_t[c]), 0.0)
        for q in range(slabs):
            sl = slice(q * LANES, (q + 1) * LANES)
            mixes = []
            for h in (2 * q, 2 * q + 1):
                gap = ct[c, :, h : h + 1] - cs[c, h : h + 1, :]
                mixes.append((jnp.exp(jnp.minimum(gap, 0.0)) * scores).astype(BF16))
            v = vals[at, sl]
            rhs = jnp.concatenate([v * first, v * second], axis=0)
            o = dot(jnp.concatenate(mixes, axis=1), rhs)
            g = grow[at, sl]
            o = o + g * dot(qc, s_loc[c, :, sl])
            mixed[at, sl] = o + skip_row[0:1, sl] * v.astype(F32)
            grow[at, sl] = g * ap[c, 0:1, sl]
        return 0

    lax.fori_loop(0, chunks, local, 0)

    def scan(b, s):
        @pl.when(b != me)
        def _():
            a_copy(b, b).wait_recv()
            f_copy(b, b).wait_recv()

        out = s.astype(BF16).reshape(seg, LANES)
        sbuf[b] = out

        @pl.when(b != me)
        def _():
            s_copy(b, me).start()

        @pl.when(b == me)
        def _():
            s_in[b] = out

        return ra[b][None] * s + rf[b].astype(F32).reshape(seg // 8, 8, LANES)

    lax.fori_loop(0, n_seq, scan, jnp.zeros((seg // 8, 8, LANES), F32))

    loads[3].wait()

    def gate(i, _):
        at = pl.ds(pl.multiple_of(i * 16, 16), 16)
        s = silu(gates[at, :].astype(F32))
        mixed[at, :] = mixed[at, :] * s
        grow[at, :] = grow[at, :] * s
        return 0

    lax.fori_loop(0, rows // 16, gate, 0)
    for load in w_loads:
        load.wait()

    def await_s(i, _):
        b = lax.rem(me + i, n_seq)
        s_copy(b, b).wait_recv()
        return 0

    lax.fori_loop(1, n_seq, await_s, 0)

    def finish_rows(m):
        top = m * half
        at = slice(top, top + half)
        qm = qs[at, :]
        total = jnp.zeros((half, LANES), F32)
        for j in range(width // 256):
            pair = [
                s_in[(2 * j + i) * split : (2 * j + i + 1) * split].reshape(128, LANES)
                for i in range(2)
            ]
            t = dot(qm, jnp.concatenate(pair, axis=1))
            sl = slice(j * 256, (j + 1) * 256)
            x = mixed[at, sl] + grow[at, sl] * t
            mixed[at, sl] = x
            total = total + x[:, :LANES] * x[:, :LANES] + x[:, LANES:] * x[:, LANES:]
        scale = lax.rsqrt(jnp.sum(total, axis=1, keepdims=True) * (1.0 / width) + EPS)
        for j in range(slabs):
            sl = slice(j * LANES, (j + 1) * LANES)
            y[at, sl] = (mixed[at, sl] * scale * gain_ref[:, sl]).astype(BF16)

    def p_copy(m, k):
        return pltpu.make_async_remote_copy(
            src_ref=p_send.at[m, k],
            dst_ref=p_recv.at[m, k],
            send_sem=p_s.at[m, k],
            recv_sem=p_r.at[m, k],
            device_id={"tp": mate},
            device_id_type=MESH,
        )

    def x_copy(send, recv, ss, rs, m, way):
        return pltpu.make_async_remote_copy(
            src_ref=send.at[m, way],
            dst_ref=recv.at[m, way],
            send_sem=ss.at[m, way],
            recv_sem=rs.at[m, way],
            device_id={"tp": ahead if way == 0 else behind},
            device_id_type=MESH,
        )

    def h_copy(m, way):
        return x_copy(h_send, h_recv, h_s, h_r, m, way)

    def d_copy(m, way):
        return x_copy(d_send, d_recv, d_s, d_r, m, way)

    def c_copy(m, way):
        return x_copy(c_send, c_recv, c_s, c_r, m, way)

    def multiply(m, k):
        at = slice(m * half, (m + 1) * half)
        p_send[m, k] = dot(y[at, :], wbuf[2 * k]).astype(BF16)
        p_copy(m, k).start()
        own[m, k] = dot(y[at, :], wbuf[2 * k + 1])

    def chip_sum(m, k, lo):
        at = slice(lo, lo + quarter)
        return own[m, k, at, :] + p_recv[m, k, at, :].astype(F32)

    def send_far(m):
        p_copy(m, 0).wait_recv()
        h_send[m, 0] = chip_sum(m, 0, 0).astype(BF16)
        h_copy(m, 0).start()
        h_send[m, 1] = chip_sum(m, 0, quarter).astype(BF16)
        h_copy(m, 1).start()

    def send_near(m, way):
        p_copy(m, 1 + way).wait_recv()
        d_send[m, way] = chip_sum(m, 1 + way, quarter if way == 0 else 0).astype(BF16)
        d_copy(m, way).start()

    def send_joined(m, way):
        h_copy(m, way).wait_recv()
        part = chip_sum(m, 1 + way, 0 if way == 0 else quarter)
        c_send[m, way] = (part + h_recv[m, way].astype(F32)).astype(BF16)
        c_copy(m, way).start()

    def close(m):
        p_copy(m, 3).wait_recv()
        for way in range(2):
            d_copy(m, 1 - way).wait_recv()
            c_copy(m, way).wait_recv()
            lo = way * quarter
            total = chip_sum(m, 3, lo)
            total = total + d_recv[m, 1 - way].astype(F32) + c_recv[m, way].astype(F32)
            out_ref[m * half + lo : m * half + lo + quarter, :] = total.astype(BF16)

    finish_rows(0)
    multiply(0, 0)
    multiply(0, 1)
    send_far(0)
    multiply(0, 2)
    send_near(0, 0)
    finish_rows(1)
    send_near(0, 1)
    multiply(1, 0)
    send_joined(0, 0)
    send_joined(0, 1)
    multiply(1, 1)
    send_far(1)
    multiply(1, 2)
    send_near(1, 0)
    multiply(0, 3)
    send_near(1, 1)
    multiply(1, 3)
    send_joined(1, 0)
    send_joined(1, 1)
    close(0)
    close(1)

    for halo in halos:
        halo.wait_send()

    def drain(i, _):
        b = lax.rem(me + i, n_seq)
        a_copy(b, me).wait_send()
        f_copy(b, me).wait_send()
        s_copy(b, me).wait_send()
        return 0

    lax.fori_loop(1, n_seq, drain, 0)
    for m in range(2):
        for k in range(4):
            p_copy(m, k).wait_send()
        for way in range(2):
            h_copy(m, way).wait_send()
            d_copy(m, way).wait_send()
            c_copy(m, way).wait_send()


def shards(
    n_seq,
    values_in,
    gates_in,
    keys_in,
    queries_in,
    log_decay,
    conv_values,
    bias_values,
    conv_keys,
    bias_keys,
    conv_queries,
    bias_queries,
    skip_scale,
    norm_gain,
    out_weight,
):
    rows, width = values_in.shape
    heads = log_decay.shape[0]
    chunks = rows // CH
    slabs = width // LANES
    seg = 128 * slabs // n_seq
    half, quarter = rows // 2, rows // 4
    depth, full = out_weight.shape
    cols = full // 8
    vmem = pl.BlockSpec(memory_space=pltpu.VMEM)
    hbm = pl.BlockSpec(memory_space=pl.ANY)
    dma = pltpu.SemaphoreType.DMA
    return pl.pallas_call(
        functools.partial(kernel, n_seq),
        out_shape=jax.ShapeDtypeStruct((rows, cols), BF16),
        in_specs=[hbm] * 4 + [vmem] * 9 + [hbm],
        out_specs=vmem,
        scratch_shapes=[
            pltpu.VMEM((rows + PAD, width + 256), BF16),
            pltpu.VMEM((rows, width), BF16),
            pltpu.VMEM((8, depth, cols), BF16),
            pltpu.VMEM((2 * heads, width), BF16),
            pltpu.VMEM((chunks, CH, heads), F32),
            pltpu.VMEM((chunks, heads, CH), F32),
            pltpu.VMEM((rows, width), F32),
            pltpu.VMEM((rows, width), F32),
            pltpu.VMEM((chunks, 8, width), F32),
            pltpu.VMEM((rows, width), BF16),
            pltpu.VMEM((CH, width), BF16),
            pltpu.VMEM((chunks, 128, CH), BF16),
            pltpu.VMEM((rows, 128), BF16),
            pltpu.VMEM((chunks, 128, width), F32),
            pltpu.VMEM((chunks, 128, width), BF16),
            pltpu.VMEM((rows, width), F32),
            pltpu.VMEM((slabs, 8, LANES), F32),
            pltpu.VMEM((n_seq, 8, LANES), F32),
            pltpu.VMEM((n_seq, seg, LANES), BF16),
            pltpu.VMEM((n_seq, seg, LANES), BF16),
            pltpu.VMEM((n_seq, seg, LANES), BF16),
            pltpu.VMEM((n_seq, seg, LANES), BF16),
            pltpu.VMEM((rows, width), BF16),
            pltpu.VMEM((2, 4, half, cols), BF16),
            pltpu.VMEM((2, 4, half, cols), BF16),
            pltpu.VMEM((2, 4, half, cols), F32),
        ]
        + [pltpu.VMEM((2, 2, quarter, cols), BF16)] * 6
        + [dma((4,)), dma((8,)), dma((3,)), dma((3,))]
        + [dma((n_seq,))] * 6
        + [dma((2, 4))] * 2
        + [dma((2, 2))] * 6,
        compiler_params=pltpu.CompilerParams(collective_id=0, has_side_effects=True),
        name="mixer",
    )(
        values_in,
        gates_in,
        keys_in,
        queries_in,
        log_decay,
        conv_values,
        bias_values[None],
        conv_keys,
        bias_keys[None],
        conv_queries,
        bias_queries[None],
        skip_scale[None],
        norm_gain[None],
        out_weight,
    )


def solution(mesh):
    placed = (
        P("seq", "tp"),
        P("seq", "tp"),
        P("seq", "tp"),
        P("seq", "tp"),
        P("tp", "seq"),
        P(None, "tp"),
        P("tp"),
        P(None, "tp"),
        P("tp"),
        P(None, "tp"),
        P("tp"),
        P("tp"),
        P("tp"),
        P("tp", None),
    )
    return jax.shard_map(
        functools.partial(shards, mesh.shape["seq"]),
        mesh=mesh,
        in_specs=placed,
        out_specs=P("seq", "tp"),
        check_vma=False,
    )
```

time: 249 us -> 60.4 us (0.24)
  waiting for transfers between devices: 101 us -> 0 us
  blocking collectives: 65.2 us -> 0 us
  Pallas kernels: 0 us -> 58.3 us
  matrix products: 39.3 us -> 0 us
  between operations: 14.3 us -> 0.01 us
  local copies, waits for them, and re-layouts: 14.4 us -> 1.87 us
  other arithmetic: 8.96 us -> 0 us
  starting transfers between devices: 4.45 us -> 0 us
    psum x1 -> x0, waiting for transfers between devices: 73.7 us -> none  [shards(): summed = lax.psum(local_sum.astype(jnp.bfloat16), 'tp').astype(jnp.float32)]
    unnamed x1 -> x0, blocking collectives: 65.2 us -> none
    pallas_call x0 -> x1, Pallas kernels: none -> 58.3 us  [shards(): pl.pallas_call(functools.partial(kernel, n_seq), out_shape=jax.ShapeDtype...]
    dot_general x7 -> x0, matrix products: 39.3 us -> none  [the longest x1 16.9 us: shards(): jnp.einsum('kh,khm->hm', jnp.exp(exponent), pieces, precision=HIGH)]
    all_gather x1 -> x0, waiting for transfers between devices: 25.7 us -> none  [shards(): lax.all_gather(flat_end[None].astype(jnp.bfloat16), 'seq', axis=0, tiled=...]
    convert_element_type x4 -> x0, other arithmetic: 4.96 us -> none  [the longest x2 2.88 us: causal_filter(): return jax.nn.silu(running).astype(jnp.bfloat16)]
    ppermute x1 -> x0, starting transfers between devices: 4.38 us -> none  [passed_along(): return lax.ppermute(block, axis, route)]
    slice x9 -> x0, local copies, waits for them, and re-layouts: 3.41 us -> none  [the longest x1 0.89 us: causal_filter(): kernel_weights[offset][None, :]]
  transfers between devices with their start and end apart: 3 -> 0, of which waited for: 3 -> 0; matrix products, arithmetic and copies ran while one was open for 7% -> 0% of each run, Pallas kernels for 0% -> 0%
where the time goes in v1:
time: 60.4 us; the launch traced here: 60.2 us
  Pallas kernels  58.3 us (97%)
  local copies, waits for them, and re-layouts  1.87 us (3%)
    pallas_call x1, Pallas kernels, shards(): pl.pallas_call(functools.partial(kernel, n_seq), out_shape=jax.ShapeDtype...  58.3 us
    unnamed x1, local copies, waits for them, and re-layouts  1.87 us

profile of v1, /device:TPU:1, one launch (start us, length us, event | category | flops | bytes accessed | tf_op | source)
XLA Modules:
  0.0 60.2 jit_solution(6905959280645970889)
XLA Ops:
  0.0 58.3 %mixer.1 = bf16[512,512]{1,0:T(8,128)(2,1)} custom-call(bf16[512,1024]{1,0:T(8,128)(2,1)} %v_hbm.1, bf16[512,1024]{1,0:T(8,128)(2,1)} %g_hbm.1, bf16[512,128]{1,0:T(8,128)(2,1)} %k_hbm.1, bf16[512,128]{1,0:T(8,128)(2,1)} %q_hbm.1, f32[16,512]{1,0:T(8,128)} %log_ref.1, f32[4,1024]{1,0:T(4,128)} %cv_ref.1, f32[1,1024]{1,0:T(1,128)} %bitcast.5, ...), custom_call_target="tpu_custom_call" | custom-call | tf_op jit(solution)/shard_map/mixer/pallas_call | solution.py:540
  58.3 1.9 %copy.16 = bf16[512,512]{1,0:T(8,128)(2,1)} copy(bf16[512,512]{1,0:T(8,128)(2,1)} %mixer.1) | data formatting | bytes 1048576

commit v2 on v1

v2 whole, which is shorter than its diff:
```python
import functools

import jax
import jax.numpy as jnp
from jax import lax
from jax.experimental import pallas as pl
from jax.experimental.pallas import tpu as pltpu
from jax.sharding import PartitionSpec as P

MESH = pl.DeviceIdType.MESH
F32 = jnp.float32
BF16 = jnp.bfloat16
EPS = 1e-05
CH = 128
PAD = 16
LANES = 128
ROW = 8


def dot(a, b):
    return jnp.dot(a, b, preferred_element_type=F32)


def silu(v):
    h = 0.5 * v
    return h + h * jnp.tanh(h)


def parts_of(x):
    hi = x.astype(BF16).astype(F32)
    rest = x - hi
    mid = rest.astype(BF16).astype(F32)
    return hi, mid, rest - mid


def kernel(
    n_seq,
    v_hbm,
    g_hbm,
    k_hbm,
    q_hbm,
    log_hbm,
    cv_hbm,
    bv_hbm,
    ck_hbm,
    bk_hbm,
    cq_hbm,
    bq_hbm,
    skip_hbm,
    gain_hbm,
    w_hbm,
    out_ref,
    log_ref,
    cv_ref,
    bv_ref,
    ck_ref,
    bk_ref,
    cq_ref,
    bq_ref,
    skip_ref,
    gain_ref,
    xpad,
    edge,
    gates,
    w_own,
    w_mate,
    spread,
    shift,
    shift_top,
    ct,
    cs,
    grow,
    rem,
    ap,
    vals,
    vw,
    keys0,
    keys_t,
    qs,
    fresh,
    rest,
    s_loc,
    mixed,
    abuf,
    ra,
    fbuf,
    rf,
    sbuf,
    s_in,
    y,
    y_mate,
    first,
    own,
    join,
    h_send,
    h_recv,
    d_send,
    d_recv,
    c_send,
    c_recv,
    small_sem,
    in_sem,
    w_sem,
    wx_s,
    wx_r,
    halo_s,
    halo_r,
    a_s,
    a_r,
    f_s,
    f_r,
    s_s,
    s_r,
    y_s,
    y_r,
    h_s,
    h_r,
    d_s,
    d_r,
    c_s,
    c_r,
):
    rows, width = v_hbm.shape
    heads = log_ref.shape[0]
    hops = sorted(
        ((dy, dz) for dy in range(n_seq // ROW) for dz in range(ROW) if dy or dz),
        key=lambda o: -min(o[0], n_seq // ROW - o[0]) - min(o[1], ROW - o[1]),
    )
    chunks = rows // CH
    slabs = width // LANES
    split = n_seq // slabs
    seg = 128 // split
    half = rows // 2
    quarter = half // 2
    tp_size = lax.axis_size("tp")
    me = lax.axis_index("seq")
    tp = lax.axis_index("tp")
    core = lax.rem(tp, 2)
    mate = tp + 1 - 2 * core
    ahead = lax.rem(tp + 2, tp_size)
    behind = lax.rem(tp + tp_size - 2, tp_size)
    far = lax.rem(tp + 4, tp_size)

    barrier = pltpu.get_barrier_semaphore()

    def greet(i, _):
        pl.semaphore_signal(
            barrier, inc=1, device_id={"seq": lax.rem(me + i, n_seq)}, device_id_type=MESH
        )
        return 0

    lax.fori_loop(1, n_seq, greet, 0)
    for other in (mate, ahead, behind):
        pl.semaphore_signal(barrier, inc=1, device_id={"tp": other}, device_id_type=MESH)

    smalls = [
        pltpu.make_async_copy(src, dst, small_sem.at[i])
        for i, (src, dst) in enumerate(
            (
                (log_hbm, log_ref),
                (cv_hbm, cv_ref),
                (bv_hbm, bv_ref),
                (ck_hbm, ck_ref),
                (bk_hbm, bk_ref),
                (cq_hbm, cq_ref),
                (bq_hbm, bq_ref),
                (skip_hbm, skip_ref),
                (gain_hbm, gain_ref),
            )
        )
    ]
    loads = [
        pltpu.make_async_copy(v_hbm, xpad.at[pl.ds(PAD, rows), pl.ds(0, width)], in_sem.at[0]),
        pltpu.make_async_copy(
            k_hbm, xpad.at[pl.ds(PAD, rows), pl.ds(width, 128)], in_sem.at[1]
        ),
        pltpu.make_async_copy(
            q_hbm, xpad.at[pl.ds(PAD, rows), pl.ds(width + 128, 128)], in_sem.at[2]
        ),
    ]
    gate_load = pltpu.make_async_copy(g_hbm, gates, in_sem.at[3])
    for load in smalls + loads:
        load.start()
    cols = w_hbm.shape[1] // tp_size

    def w_part(k, side):
        chip = (far, ahead, behind, tp)[k] - core
        return w_hbm.at[:, pl.ds(pl.multiple_of((chip + side) * cols, cols), cols)]

    w_loads = [
        pltpu.make_async_copy(w_part(k, core), w_own.at[k], w_sem.at[k]) for k in range(4)
    ]

    def w_copy(k):
        return pltpu.make_async_remote_copy(
            src_ref=w_part(k, 1 - core),
            dst_ref=w_mate.at[k],
            send_sem=wx_s.at[k],
            recv_sem=wx_r.at[k],
            device_id={"tp": mate},
            device_id_type=MESH,
        )

    xpad[0:PAD, :] = jnp.zeros((PAD, xpad.shape[1]), BF16)
    for ref, span in ((shift, CH), (shift_top, PAD)):
        out_row = lax.broadcasted_iota(jnp.int32, ref.shape, 0)
        in_row = lax.broadcasted_iota(jnp.int32, ref.shape, 1)
        hit = out_row == -1
        for back in range(1, 4):
            base = (back - 1) * span
            here = (out_row >= base) & (out_row < base + span)
            hit = hit | (here & (in_row == out_row - base + PAD - back))
        ref[...] = jnp.where(hit, 1.0, 0.0).astype(BF16)

    lane_head = lax.broadcasted_iota(jnp.int32, (2 * heads, width), 1) // (width // heads)
    row_head = lax.broadcasted_iota(jnp.int32, (2 * heads, width), 0)
    row_head = jnp.where(row_head >= heads, row_head - heads, row_head)
    spread[...] = jnp.where(lane_head == row_head, 1.0, 0.0).astype(BF16)

    def expand(x):
        hi = x.astype(BF16).astype(F32)
        return jnp.concatenate([hi, x - hi], axis=1).astype(BF16)

    low_a = lax.broadcasted_iota(jnp.int32, (CH, CH), 0)
    low_b = lax.broadcasted_iota(jnp.int32, (CH, CH), 1)
    lower = jnp.where(low_b <= low_a, 1.0, 0.0)
    lower3 = jnp.concatenate([lower] * 3, axis=1).astype(BF16)
    upper = jnp.where(low_a <= low_b, 1.0, 0.0)
    upper3 = jnp.concatenate([upper] * 3, axis=0).astype(BF16)

    def decay(c, _):
        at = pl.ds(pl.multiple_of(c * CH, CH), CH)
        logs = jnp.concatenate(parts_of(log_ref[:, at]), axis=1).astype(BF16)
        col = lax.dot_general(lower3, logs, (((1,), (1,)), ((), ())), preferred_element_type=F32)
        ct[c] = col
        cs[c] = dot(logs, upper3)
        g2 = expand(jnp.exp(col))
        r2 = expand(jnp.exp(jnp.minimum(col[CH - 1 : CH, :] - col, 0.0)))
        for j in range(width // 256):
            sl = slice(j * 256, (j + 1) * 256)
            grow[at, sl] = dot(g2, spread[:, sl])
            rem[at, sl] = dot(r2, spread[:, sl])
        return 0

    smalls[0].wait()
    lax.fori_loop(0, chunks, decay, 0)
    before = jnp.ones((1, width), F32)
    for c in range(chunks):
        ap[c] = jnp.broadcast_to(before, (8, width))
        before = before * grow[c * CH + CH - 1 : c * CH + CH, :]
    for q in range(slabs):
        abuf[q] = jnp.broadcast_to(before[:, q * LANES : (q + 1) * LANES], (8, LANES))
    after = {"seq": lax.rem(me + 1, n_seq)}
    halos = []
    for i, (src, lo, wid) in enumerate(
        ((v_hbm, 0, width), (k_hbm, width, 128), (q_hbm, width + 128, 128))
    ):
        halos.append(
            pltpu.make_async_remote_copy(
                src_ref=src.at[pl.ds(rows - PAD, PAD), :],
                dst_ref=edge.at[:, pl.ds(lo, wid)],
                send_sem=halo_s.at[i],
                recv_sem=halo_r.at[i],
                device_id=after,
                device_id_type=MESH,
            )
        )

    def a_copy(peer, slot):
        return pltpu.make_async_remote_copy(
            src_ref=abuf.at[peer // split],
            dst_ref=ra.at[slot],
            send_sem=a_s.at[peer],
            recv_sem=a_r.at[slot],
            device_id={"seq": peer},
            device_id_type=MESH,
        )

    def f_copy(peer, slot):
        return pltpu.make_async_remote_copy(
            src_ref=fbuf.at[peer],
            dst_ref=rf.at[slot],
            send_sem=f_s.at[peer],
            recv_sem=f_r.at[slot],
            device_id={"seq": peer},
            device_id_type=MESH,
        )

    def s_copy(peer, slot):
        return pltpu.make_async_remote_copy(
            src_ref=sbuf.at[peer],
            dst_ref=s_in.at[slot],
            send_sem=s_s.at[peer],
            recv_sem=s_r.at[slot],
            device_id={"seq": peer},
            device_id_type=MESH,
        )

    def send_a(i, _):
        a_copy(lax.rem(me + i, n_seq), me).start()
        return 0

    def taps(x, shifted, span, w_ref, b_ref, sl):
        acc = b_ref[:, sl] + w_ref[3:4, sl] * x.astype(F32)
        for back in range(1, 4):
            acc = acc + w_ref[3 - back : 4 - back, sl] * shifted[(back - 1) * span : back * span]
        return silu(acc).astype(BF16)

    def conv(c, top):
        at = pl.ds(pl.multiple_of(c * CH, CH), CH)
        window = pl.ds(pl.multiple_of(c * CH, CH), CH + PAD)
        kq = slice(width, width + 256)
        x = xpad[window, kq]
        moved = dot(shift[...], x)
        one = slice(0, 128)
        keys = taps(x[PAD:, :128], moved[:, :128], CH, ck_ref, bk_ref, one)
        kt = keys.astype(F32).T.astype(BF16)
        keys_t[c] = kt
        if top:
            keys0[...] = keys
        qs[at, :] = taps(x[PAD:, 128:], moved[:, 128:], CH, cq_ref, bq_ref, one)
        for j in range(width // 256):
            sl = slice(j * 256, (j + 1) * 256)
            x = xpad[window, sl]
            v = taps(x[PAD:], dot(shift[...], x), CH, cv_ref, bv_ref, sl)
            vals[at, sl] = v
            weighted = (v.astype(F32) * rem[at, sl]).astype(BF16)
            if top:
                vw[:, sl] = weighted
                vw[0:PAD, sl] = jnp.zeros((PAD, 256), BF16)
                weighted = vw[:, sl]
            fresh[c, :, sl] = dot(kt, weighted)

    for load in smalls[1:] + loads:
        load.wait()
    gate_load.start()
    for load in w_loads:
        load.start()

    def conv_step(i, _):
        conv(chunks - i, False)
        return 0

    lax.fori_loop(1, 3, conv_step, 0)

    pl.semaphore_wait(barrier, n_seq - 1 + 3)
    for halo in halos:
        halo.start()
    lax.fori_loop(1, n_seq, send_a, 0)
    ra[me] = abuf[me // split]
    for k in range(4):
        w_copy(k).start()

    lax.fori_loop(3, chunks, conv_step, 0)
    conv(0, True)
    for q in range(slabs):
        sl = slice(q * LANES, (q + 1) * LANES)
        s = fresh[0, :, sl]
        for c in range(1, chunks):
            s = grow[c * CH + CH - 1 : c * CH + CH, sl] * s + fresh[c, :, sl]
        rest[:, sl] = s

    later = jnp.ones((1, width), F32)
    for c in range(1, chunks):
        later = later * grow[c * CH + CH - 1 : c * CH + CH, :]
    is_first = me == 0
    for halo in halos:
        halo.wait_recv()
    head = slice(0, PAD)

    def top_rows(sl):
        above = jnp.where(is_first, 0.0, edge[:, sl].astype(F32)).astype(BF16)
        here = xpad[PAD : 2 * PAD, sl]
        return here, dot(shift_top[...], jnp.concatenate([above, here], axis=0))

    x, moved = top_rows(slice(width, width + 256))
    keys0[head, :] = taps(x[:, :128], moved[:, :128], PAD, ck_ref, bk_ref, slice(0, 128))
    qs[head, :] = taps(x[:, 128:], moved[:, 128:], PAD, cq_ref, bq_ref, slice(0, 128))
    kt = keys0[...].astype(F32).T.astype(BF16)
    keys_t[0] = kt
    for j in range(width // 256):
        sl = slice(j * 256, (j + 1) * 256)
        x, moved = top_rows(sl)
        v = taps(x, moved, PAD, cv_ref, bv_ref, sl)
        vals[head, sl] = v
        weighted = (v.astype(F32) * rem[head, sl]).astype(BF16)
        more = dot(kt[:, :PAD], weighted)
        fresh[0, :, sl] = fresh[0, :, sl] + more
        f = (rest[:, sl] + later[:, sl] * more).astype(BF16)
        for i in range(2):
            for r in range(split):
                fbuf[(2 * j + i) * split + r] = f[
                    r * seg : (r + 1) * seg, i * LANES : (i + 1) * LANES
                ]

    def far_first(copy):
        for dy, dz in hops:
            at = lax.rem(me // ROW + dy, n_seq // ROW) * ROW + lax.rem(lax.rem(me, ROW) + dz, ROW)
            copy(at, me).start()

    far_first(f_copy)
    rf[me] = fbuf[me]

    for q in range(slabs):
        sl = slice(q * LANES, (q + 1) * LANES)
        s = fresh[0, :, sl]
        s_loc[0, :, sl] = jnp.zeros((128, LANES), BF16)
        for c in range(1, chunks):
            s_loc[c, :, sl] = s.astype(BF16)
            s = grow[c * CH + CH - 1 : c * CH + CH, sl] * s + fresh[c, :, sl]

    skip8 = jnp.broadcast_to(skip_ref[...], (8, heads))
    skip_row = dot(expand(skip8), spread[...])
    lane = lax.broadcasted_iota(jnp.int32, (1, LANES), 1)
    front = jnp.where(lane < LANES // 2, 1.0, 0.0).astype(BF16)
    back_half = jnp.where(lane < LANES // 2, 0.0, 1.0).astype(BF16)

    def local(c, _):
        at = pl.ds(pl.multiple_of(c * CH, CH), CH)
        qc = qs[at, :]
        scores = jnp.where(low_b <= low_a, dot(qc, keys_t[c]), 0.0)
        for q in range(slabs):
            sl = slice(q * LANES, (q + 1) * LANES)
            mixes = []
            for h in (2 * q, 2 * q + 1):
                gap = ct[c, :, h : h + 1] - cs[c, h : h + 1, :]
                mixes.append((jnp.exp(jnp.minimum(gap, 0.0)) * scores).astype(BF16))
            v = vals[at, sl]
            rhs = jnp.concatenate([v * front, v * back_half], axis=0)
            o = dot(jnp.concatenate(mixes, axis=1), rhs)
            g = grow[at, sl]
            o = o + g * dot(qc, s_loc[c, :, sl])
            mixed[at, sl] = o + skip_row[0:1, sl] * v.astype(F32)
            grow[at, sl] = g * ap[c, 0:1, sl]
        return 0

    lax.fori_loop(0, chunks, local, 0)

    def await_f(i, _):
        b = lax.rem(me + i, n_seq)
        a_copy(b, b).wait_recv()
        f_copy(b, b).wait_recv()
        return 0

    lax.fori_loop(1, n_seq, await_f, 0)
    state = jnp.zeros((seg // 8, 8, LANES), F32)
    for b in range(n_seq):
        sbuf[b] = state.astype(BF16).reshape(seg, LANES)
        state = ra[b][None] * state + rf[b].astype(F32).reshape(seg // 8, 8, LANES)
    far_first(s_copy)
    s_in[me] = sbuf[me]

    gate_load.wait()

    def gate(i, _):
        at = pl.ds(pl.multiple_of(i * 16, 16), 16)
        s = silu(gates[at, :].astype(F32))
        mixed[at, :] = mixed[at, :] * s
        grow[at, :] = grow[at, :] * s
        return 0

    lax.fori_loop(0, rows // 16, gate, 0)
    for load in w_loads:
        load.wait()
    for k in range(4):
        w_copy(k).wait_recv()

    def await_s(i, _):
        b = lax.rem(me + i, n_seq)
        s_copy(b, b).wait_recv()
        return 0

    lax.fori_loop(1, n_seq, await_s, 0)

    def y_copy(p):
        return pltpu.make_async_remote_copy(
            src_ref=y.at[p],
            dst_ref=y_mate.at[p],
            send_sem=y_s.at[p],
            recv_sem=y_r.at[p],
            device_id={"tp": mate},
            device_id_type=MESH,
        )

    def finish_rows(p):
        at = slice(p * quarter, (p + 1) * quarter)
        qm = qs[at, :]
        total = jnp.zeros((quarter, LANES), F32)
        for j in range(width // 256):
            pair = [
                s_in[(2 * j + i) * split : (2 * j + i + 1) * split].reshape(128, LANES)
                for i in range(2)
            ]
            t = dot(qm, jnp.concatenate(pair, axis=1))
            sl = slice(j * 256, (j + 1) * 256)
            x = mixed[at, sl] + grow[at, sl] * t
            mixed[at, sl] = x
            total = total + x[:, :LANES] * x[:, :LANES] + x[:, LANES:] * x[:, LANES:]
        scale = lax.rsqrt(jnp.sum(total, axis=1, keepdims=True) * (1.0 / width) + EPS)
        for j in range(slabs):
            sl = slice(j * LANES, (j + 1) * LANES)
            y[p, :, sl] = (mixed[at, sl] * scale * gain_ref[:, sl]).astype(BF16)
        y_copy(p).start()

    def x_copy(send, recv, ss, rs, m, way):
        return pltpu.make_async_remote_copy(
            src_ref=send.at[m, way],
            dst_ref=recv.at[m, way],
            send_sem=ss.at[m, way],
            recv_sem=rs.at[m, way],
            device_id={"tp": ahead if way == 0 else behind},
            device_id_type=MESH,
        )

    def h_copy(m, way):
        return x_copy(h_send, h_recv, h_s, h_r, m, way)

    def d_copy(m, way):
        return x_copy(d_send, d_recv, d_s, d_r, m, way)

    def c_copy(m, way):
        return x_copy(c_send, c_recv, c_s, c_r, m, way)

    def chip_sum(m, k):
        rows_own = y[2 * m : 2 * m + 2].reshape(half, width)
        rows_mate = y_mate[2 * m : 2 * m + 2].reshape(half, width)
        return dot(rows_own, w_own[k]) + dot(rows_mate, w_mate[k])

    for p in range(4):
        finish_rows(p)
    for p in range(4):
        first[p] = dot(y[p], w_own[0])
    for p in range(4):
        y_copy(p).wait_recv()
        h_send[p // 2, p % 2] = (first[p] + dot(y_mate[p], w_mate[0])).astype(BF16)
        h_copy(p // 2, p % 2).start()
    for m in range(2):
        for way in range(2):
            total = chip_sum(m, 1 + way)
            parts = total[:quarter], total[quarter:]
            d_send[m, way] = parts[1 - way].astype(BF16)
            d_copy(m, way).start()
            join[m, way] = parts[way]
    for m in range(2):
        own[m] = chip_sum(m, 3)
    for m in range(2):
        for way in range(2):
            h_copy(m, way).wait_recv()
            c_send[m, way] = (join[m, way] + h_recv[m, way].astype(F32)).astype(BF16)
            c_copy(m, way).start()
    for m in range(2):
        for way in range(2):
            d_copy(m, 1 - way).wait_recv()
            c_copy(m, way).wait_recv()
            lo = way * quarter
            total = own[m, lo : lo + quarter, :]
            total = total + d_recv[m, 1 - way].astype(F32) + c_recv[m, way].astype(F32)
            out_ref[m * half + lo : m * half + lo + quarter, :] = total.astype(BF16)

    for halo in halos:
        halo.wait_send()

    def drain(i, _):
        b = lax.rem(me + i, n_seq)
        a_copy(b, me).wait_send()
        f_copy(b, me).wait_send()
        s_copy(b, me).wait_send()
        return 0

    lax.fori_loop(1, n_seq, drain, 0)
    for k in range(4):
        w_copy(k).wait_send()
        y_copy(k).wait_send()
    for m in range(2):
        for way in range(2):
            h_copy(m, way).wait_send()
            d_copy(m, way).wait_send()
            c_copy(m, way).wait_send()


def shards(
    n_seq,
    values_in,
    gates_in,
    keys_in,
    queries_in,
    log_decay,
    conv_values,
    bias_values,
    conv_keys,
    bias_keys,
    conv_queries,
    bias_queries,
    skip_scale,
    norm_gain,
    out_weight,
):
    rows, width = values_in.shape
    heads = log_decay.shape[0]
    chunks = rows // CH
    slabs = width // LANES
    seg = 128 * slabs // n_seq
    half, quarter = rows // 2, rows // 4
    depth, full = out_weight.shape
    cols = full // 8
    hbm = pl.BlockSpec(memory_space=pl.ANY)
    dma = pltpu.SemaphoreType.DMA
    args = (
        values_in,
        gates_in,
        keys_in,
        queries_in,
        log_decay,
        conv_values,
        bias_values[None],
        conv_keys,
        bias_keys[None],
        conv_queries,
        bias_queries[None],
        skip_scale[None],
        norm_gain[None],
        out_weight,
    )
    return pl.pallas_call(
        functools.partial(kernel, n_seq),
        out_shape=jax.ShapeDtypeStruct((rows, cols), BF16),
        in_specs=[hbm] * len(args),
        out_specs=pl.BlockSpec(memory_space=pltpu.VMEM),
        scratch_shapes=[pltpu.VMEM(a.shape, a.dtype) for a in args[4:13]]
        + [
            pltpu.VMEM((rows + PAD, width + 256), BF16),
            pltpu.VMEM((PAD, width + 256), BF16),
            pltpu.VMEM((rows, width), BF16),
            pltpu.VMEM((4, depth, cols), BF16),
            pltpu.VMEM((4, depth, cols), BF16),
            pltpu.VMEM((2 * heads, width), BF16),
            pltpu.VMEM((3 * CH, CH + PAD), BF16),
            pltpu.VMEM((3 * PAD, 2 * PAD), BF16),
            pltpu.VMEM((chunks, CH, heads), F32),
            pltpu.VMEM((chunks, heads, CH), F32),
            pltpu.VMEM((rows, width), F32),
            pltpu.VMEM((rows, width), F32),
            pltpu.VMEM((chunks, 8, width), F32),
            pltpu.VMEM((rows, width), BF16),
            pltpu.VMEM((CH, width), BF16),
            pltpu.VMEM((CH, 128), BF16),
            pltpu.VMEM((chunks, 128, CH), BF16),
            pltpu.VMEM((rows, 128), BF16),
            pltpu.VMEM((chunks, 128, width), F32),
            pltpu.VMEM((128, width), F32),
            pltpu.VMEM((chunks, 128, width), BF16),
            pltpu.VMEM((rows, width), F32),
            pltpu.VMEM((slabs, 8, LANES), F32),
            pltpu.VMEM((n_seq, 8, LANES), F32),
            pltpu.VMEM((n_seq, seg, LANES), BF16),
            pltpu.VMEM((n_seq, seg, LANES), BF16),
            pltpu.VMEM((n_seq, seg, LANES), BF16),
            pltpu.VMEM((n_seq, seg, LANES), BF16),
            pltpu.VMEM((4, quarter, width), BF16),
            pltpu.VMEM((4, quarter, width), BF16),
            pltpu.VMEM((4, quarter, cols), F32),
            pltpu.VMEM((2, half, cols), F32),
            pltpu.VMEM((2, 2, quarter, cols), F32),
        ]
        + [pltpu.VMEM((2, 2, quarter, cols), BF16)] * 6
        + [dma((9,)), dma((4,)), dma((4,)), dma((4,)), dma((4,)), dma((3,)), dma((3,))]
        + [dma((n_seq,))] * 6
        + [dma((4,))] * 2
        + [dma((2, 2))] * 6,
        compiler_params=pltpu.CompilerParams(
            collective_id=0, has_side_effects=True, vmem_limit_bytes=48 * 2**20
        ),
        name="mixer",
    )(*[pltpu.with_memory_space_constraint(a, pltpu.HBM) for a in args])


def solution(mesh):
    placed = (
        P("seq", "tp"),
        P("seq", "tp"),
        P("seq", "tp"),
        P("seq", "tp"),
        P("tp", "seq"),
        P(None, "tp"),
        P("tp"),
        P(None, "tp"),
        P("tp"),
        P(None, "tp"),
        P("tp"),
        P("tp"),
        P("tp"),
        P("tp", None),
    )
    return jax.shard_map(
        functools.partial(shards, mesh.shape["seq"]),
        mesh=mesh,
        in_specs=placed,
        out_specs=P("seq", "tp"),
        check_vma=False,
    )
```

time: 60.4 us -> 58 us (0.960)
  Pallas kernels: 58.3 us -> 57.1 us
  local copies, waits for them, and re-layouts: 1.87 us -> 0.8 us
    pallas_call x1, Pallas kernels: 58.3 us -> 57.1 us  [shards(): pl.pallas_call(functools.partial(kernel, n_seq), out_shape=jax.ShapeDtype...]
    unnamed x1, local copies, waits for them, and re-layouts: 1.87 us -> 0.8 us
where the time goes in v2:
time: 58 us; the launch traced here: 57.9 us
  Pallas kernels  57.1 us (98%)
  local copies, waits for them, and re-layouts  0.8 us (1%)
    pallas_call x1, Pallas kernels, shards(): pl.pallas_call(functools.partial(kernel, n_seq), out_shape=jax.ShapeDtype...  57.1 us

profile of v2, /device:TPU:1, one launch (start us, length us, event | category | flops | bytes accessed | tf_op | source)
XLA Modules:
  0.0 57.9 jit_solution(4099677010179454752)
XLA Ops:
  0.0 57.1 %mixer.1 = bf16[512,512]{1,0:T(8,128)(2,1)S(1)} custom-call(bf16[512,1024]{1,0:T(8,128)(2,1)} %v_hbm.1, bf16[512,1024]{1,0:T(8,128)(2,1)} %g_hbm.1, bf16[512,128]{1,0:T(8,128)(2,1)} %k_hbm.1, bf16[512,128]{1,0:T(8,128)(2,1)} %q_hbm.1, f32[16,512]{1,0:T(8,128)} %log_hbm.1, f32[4,1024]{1,0:T(4,128)} %cv_hbm.1, f32[1,1024]{1,0:T(1,128)} %bitcast.5, ...), custom_call_target="tpu_custom_call" | custom-call | tf_op jit(solution)/shard_map/mixer/pallas_call | solution.py:624
  57.1 0.8 %copy.16 = bf16[512,512]{1,0:T(8,128)(2,1)} copy(bf16[512,512]{1,0:T(8,128)(2,1)S(1)} %mixer.1) | data formatting | bytes 1048576

commit v3 on v2

--- a/solution.py
+++ b/solution.py
@@ -65,12 +65,12 @@
     w_own,
     w_mate,
     spread,
-    shift,
     shift_top,
     ct,
     cs,
     grow,
     rem,
+    dec,
     ap,
     vals,
     vw,
@@ -107,6 +107,8 @@
     halo_r,
     a_s,
     a_r,
+    b_s,
+    b_r,
     f_s,
     f_r,
     s_s,
@@ -202,7 +204,7 @@
         )
 
     xpad[0:PAD, :] = jnp.zeros((PAD, xpad.shape[1]), BF16)
-    for ref, span in ((shift, CH), (shift_top, PAD)):
+    for ref, span in ((shift_top, PAD),):
         out_row = lax.broadcasted_iota(jnp.int32, ref.shape, 0)
         in_row = lax.broadcasted_iota(jnp.int32, ref.shape, 1)
         hit = out_row == -1
@@ -234,11 +236,11 @@
         col = lax.dot_general(lower3, logs, (((1,), (1,)), ((), ())), preferred_element_type=F32)
         ct[c] = col
         cs[c] = dot(logs, upper3)
-        g2 = expand(jnp.exp(col))
+        last = expand(jnp.exp(col[CH - 8 :, :]))
         r2 = expand(jnp.exp(jnp.minimum(col[CH - 1 : CH, :] - col, 0.0)))
         for j in range(width // 256):
             sl = slice(j * 256, (j + 1) * 256)
-            grow[at, sl] = dot(g2, spread[:, sl])
+            dec[c, :, sl] = dot(last, spread[:, sl])
             rem[at, sl] = dot(r2, spread[:, sl])
         return 0
 
@@ -247,9 +249,9 @@
     before = jnp.ones((1, width), F32)
     for c in range(chunks):
         ap[c] = jnp.broadcast_to(before, (8, width))
-        before = before * grow[c * CH + CH - 1 : c * CH + CH, :]
+        before = before * dec[c, 7:8, :]
     for q in range(slabs):
-        abuf[q] = jnp.broadcast_to(before[:, q * LANES : (q + 1) * LANES], (8, LANES))
+        abuf[q : q + 1, :] = before[:, q * LANES : (q + 1) * LANES]
     after = {"seq": lax.rem(me + 1, n_seq)}
     halos = []
     for i, (src, lo, wid) in enumerate(
@@ -266,13 +268,26 @@
             )
         )
 
-    def a_copy(peer, slot):
+    row, col = me // ROW, lax.rem(me, ROW)
+
+    def a_copy(i):
         return pltpu.make_async_remote_copy(
-            src_ref=abuf.at[peer // split],
-            dst_ref=ra.at[slot],
-            send_sem=a_s.at[peer],
-            recv_sem=a_r.at[slot],
-            device_id={"seq": peer},
+            src_ref=abuf,
+            dst_ref=ra.at[me],
+            send_sem=a_s.at[i],
+            recv_sem=a_r.at[i],
+            device_id={"seq": row * ROW + lax.rem(col + i, ROW)},
+            device_id_type=MESH,
+        )
+
+    def b_copy(i):
+        mine = pl.ds(pl.multiple_of(row * ROW, ROW), ROW)
+        return pltpu.make_async_remote_copy(
+            src_ref=ra.at[mine],
+            dst_ref=ra.at[mine],
+            send_sem=b_s.at[i],
+            recv_sem=b_r.at[i],
+            device_id={"seq": lax.rem(row + i, n_seq // ROW) * ROW + col},
             device_id_type=MESH,
         )
 
@@ -296,40 +311,39 @@
             device_id_type=MESH,
         )
 
-    def send_a(i, _):
-        a_copy(lax.rem(me + i, n_seq), me).start()
-        return 0
-
     def taps(x, shifted, span, w_ref, b_ref, sl):
         acc = b_ref[:, sl] + w_ref[3:4, sl] * x.astype(F32)
         for back in range(1, 4):
             acc = acc + w_ref[3 - back : 4 - back, sl] * shifted[(back - 1) * span : back * span]
         return silu(acc).astype(BF16)
 
+    def rolled(window, lo, w_ref, b_ref, sl):
+        x = xpad[window, lo : lo + LANES].astype(F32)
+        acc = b_ref[:, sl] + w_ref[3:4, sl] * x[PAD:]
+        for back in range(1, 4):
+            acc = acc + w_ref[3 - back : 4 - back, sl] * pltpu.roll(x, back, axis=0)[PAD:]
+        return silu(acc).astype(BF16)
+
     def conv(c, top):
         at = pl.ds(pl.multiple_of(c * CH, CH), CH)
         window = pl.ds(pl.multiple_of(c * CH, CH), CH + PAD)
-        kq = slice(width, width + 256)
-        x = xpad[window, kq]
-        moved = dot(shift[...], x)
         one = slice(0, 128)
-        keys = taps(x[PAD:, :128], moved[:, :128], CH, ck_ref, bk_ref, one)
+        keys = rolled(window, width, ck_ref, bk_ref, one)
         kt = keys.astype(F32).T.astype(BF16)
         keys_t[c] = kt
         if top:
             keys0[...] = keys
-        qs[at, :] = taps(x[PAD:, 128:], moved[:, 128:], CH, cq_ref, bq_ref, one)
+        qs[at, :] = rolled(window, width + 128, cq_ref, bq_ref, one)
+        for j in range(slabs):
+            sl = slice(j * LANES, (j + 1) * LANES)
+            v = rolled(window, j * LANES, cv_ref, bv_ref, sl)
+            vals[at, sl] = v
+            vw[:, sl] = (v.astype(F32) * rem[at, sl]).astype(BF16)
+            if top:
+                vw[0:PAD, sl] = jnp.zeros((PAD, LANES), BF16)
         for j in range(width // 256):
             sl = slice(j * 256, (j + 1) * 256)
-            x = xpad[window, sl]
-            v = taps(x[PAD:], dot(shift[...], x), CH, cv_ref, bv_ref, sl)
-            vals[at, sl] = v
-            weighted = (v.astype(F32) * rem[at, sl]).astype(BF16)
-            if top:
-                vw[:, sl] = weighted
-                vw[0:PAD, sl] = jnp.zeros((PAD, 256), BF16)
-                weighted = vw[:, sl]
-            fresh[c, :, sl] = dot(kt, weighted)
+            fresh[c, :, sl] = dot(kt, vw[:, sl])
 
     for load in smalls[1:] + loads:
         load.wait()
@@ -346,8 +360,9 @@
     pl.semaphore_wait(barrier, n_seq - 1 + 3)
     for halo in halos:
         halo.start()
-    lax.fori_loop(1, n_seq, send_a, 0)
-    ra[me] = abuf[me // split]
+    for i in range(1, ROW):
+        a_copy(i).start()
+    ra[me] = abuf[...]
     for k in range(4):
         w_copy(k).start()
 
@@ -357,12 +372,12 @@
         sl = slice(q * LANES, (q + 1) * LANES)
         s = fresh[0, :, sl]
         for c in range(1, chunks):
-            s = grow[c * CH + CH - 1 : c * CH + CH, sl] * s + fresh[c, :, sl]
+            s = dec[c, 7:8, sl] * s + fresh[c, :, sl]
         rest[:, sl] = s
 
     later = jnp.ones((1, width), F32)
     for c in range(1, chunks):
-        later = later * grow[c * CH + CH - 1 : c * CH + CH, :]
+        later = later * dec[c, 7:8, :]
     is_first = me == 0
     for halo in halos:
         halo.wait_recv()
@@ -400,6 +415,10 @@
 
     far_first(f_copy)
     rf[me] = fbuf[me]
+    for i in range(1, ROW):
+        a_copy(i).wait_recv()
+    for i in range(1, n_seq // ROW):
+        b_copy(i).start()
 
     for q in range(slabs):
         sl = slice(q * LANES, (q + 1) * LANES)
@@ -407,7 +426,7 @@
         s_loc[0, :, sl] = jnp.zeros((128, LANES), BF16)
         for c in range(1, chunks):
             s_loc[c, :, sl] = s.astype(BF16)
-            s = grow[c * CH + CH - 1 : c * CH + CH, sl] * s + fresh[c, :, sl]
+            s = dec[c, 7:8, sl] * s + fresh[c, :, sl]
 
     skip8 = jnp.broadcast_to(skip_ref[...], (8, heads))
     skip_row = dot(expand(skip8), spread[...])
@@ -418,6 +437,7 @@
     def local(c, _):
         at = pl.ds(pl.multiple_of(c * CH, CH), CH)
         qc = qs[at, :]
+        g2 = expand(jnp.exp(ct[c]))
         scores = jnp.where(low_b <= low_a, dot(qc, keys_t[c]), 0.0)
         for q in range(slabs):
             sl = slice(q * LANES, (q + 1) * LANES)
@@ -428,7 +448,7 @@
             v = vals[at, sl]
             rhs = jnp.concatenate([v * front, v * back_half], axis=0)
             o = dot(jnp.concatenate(mixes, axis=1), rhs)
-            g = grow[at, sl]
+            g = dot(g2, spread[:, sl])
             o = o + g * dot(qc, s_loc[c, :, sl])
             mixed[at, sl] = o + skip_row[0:1, sl] * v.astype(F32)
             grow[at, sl] = g * ap[c, 0:1, sl]
@@ -438,15 +458,16 @@
 
     def await_f(i, _):
         b = lax.rem(me + i, n_seq)
-        a_copy(b, b).wait_recv()
         f_copy(b, b).wait_recv()
         return 0
 
     lax.fori_loop(1, n_seq, await_f, 0)
+    for i in range(1, n_seq // ROW):
+        b_copy(i).wait_recv()
     state = jnp.zeros((seg // 8, 8, LANES), F32)
     for b in range(n_seq):
         sbuf[b] = state.astype(BF16).reshape(seg, LANES)
-        state = ra[b][None] * state + rf[b].astype(F32).reshape(seg // 8, 8, LANES)
+        state = ra[b, pl.ds(me // split, 1), :][None] * state + rf[b].astype(F32).reshape(seg // 8, 8, LANES)
     far_first(s_copy)
     s_in[me] = sbuf[me]
 
@@ -500,7 +521,6 @@
         for j in range(slabs):
             sl = slice(j * LANES, (j + 1) * LANES)
             y[p, :, sl] = (mixed[at, sl] * scale * gain_ref[:, sl]).astype(BF16)
-        y_copy(p).start()
 
     def x_copy(send, recv, ss, rs, m, way):
         return pltpu.make_async_remote_copy(
@@ -528,9 +548,16 @@
 
     for p in range(4):
         finish_rows(p)
+        if p < 2:
+            y_copy(p).start()
     for p in range(4):
         first[p] = dot(y[p], w_own[0])
     for p in range(4):
+        if p == 0:
+            y_copy(0).wait_send()
+            y_copy(1).wait_send()
+            y_copy(2).start()
+            y_copy(3).start()
         y_copy(p).wait_recv()
         h_send[p // 2, p % 2] = (first[p] + dot(y_mate[p], w_mate[0])).astype(BF16)
         h_copy(p // 2, p % 2).start()
@@ -562,15 +589,19 @@
 
     def drain(i, _):
         b = lax.rem(me + i, n_seq)
-        a_copy(b, me).wait_send()
         f_copy(b, me).wait_send()
         s_copy(b, me).wait_send()
         return 0
 
     lax.fori_loop(1, n_seq, drain, 0)
+    for i in range(1, ROW):
+        a_copy(i).wait_send()
+    for i in range(1, n_seq // ROW):
+        b_copy(i).wait_send()
     for k in range(4):
         w_copy(k).wait_send()
-        y_copy(k).wait_send()
+    for p in range(2, 4):
+        y_copy(p).wait_send()
     for m in range(2):
         for way in range(2):
             h_copy(m, way).wait_send()
@@ -634,12 +665,12 @@
             pltpu.VMEM((4, depth, cols), BF16),
             pltpu.VMEM((4, depth, cols), BF16),
             pltpu.VMEM((2 * heads, width), BF16),
-            pltpu.VMEM((3 * CH, CH + PAD), BF16),
             pltpu.VMEM((3 * PAD, 2 * PAD), BF16),
             pltpu.VMEM((chunks, CH, heads), F32),
             pltpu.VMEM((chunks, heads, CH), F32),
             pltpu.VMEM((rows, width), F32),
             pltpu.VMEM((rows, width), F32),
+            pltpu.VMEM((chunks, 8, width), F32),
             pltpu.VMEM((chunks, 8, width), F32),
             pltpu.VMEM((rows, width), BF16),
             pltpu.VMEM((CH, width), BF16),
@@ -650,8 +681,8 @@
             pltpu.VMEM((128, width), F32),
             pltpu.VMEM((chunks, 128, width), BF16),
             pltpu.VMEM((rows, width), F32),
-            pltpu.VMEM((slabs, 8, LANES), F32),
-            pltpu.VMEM((n_seq, 8, LANES), F32),
+            pltpu.VMEM((slabs, LANES), F32),
+            pltpu.VMEM((n_seq, slabs, LANES), F32),
             pltpu.VMEM((n_seq, seg, LANES), BF16),
             pltpu.VMEM((n_seq, seg, LANES), BF16),
             pltpu.VMEM((n_seq, seg, LANES), BF16),
@@ -664,7 +695,9 @@
         ]
         + [pltpu.VMEM((2, 2, quarter, cols), BF16)] * 6
         + [dma((9,)), dma((4,)), dma((4,)), dma((4,)), dma((4,)), dma((3,)), dma((3,))]
-        + [dma((n_seq,))] * 6
+        + [dma((ROW,))] * 2
+        + [dma((n_seq // ROW,))] * 2
+        + [dma((n_seq,))] * 4
         + [dma((4,))] * 2
         + [dma((2, 2))] * 6,
         compiler_params=pltpu.CompilerParams(

time: 58 us -> 56.8 us (0.979)
  Pallas kernels: 57.1 us -> 55.9 us
    pallas_call x1, Pallas kernels: 57.1 us -> 55.9 us  [shards(): pl.pallas_call(functools.partial(kernel, n_seq), out_shape=jax.ShapeDtype...]
where the time goes in v3:
time: 56.8 us; the launch traced here: 56.7 us
  Pallas kernels  55.9 us (98%)
  local copies, waits for them, and re-layouts  0.8 us (1%)
    pallas_call x1, Pallas kernels, shards(): pl.pallas_call(functools.partial(kernel, n_seq), out_shape=jax.ShapeDtype...  55.9 us

profile of v3, /device:TPU:1, one launch (start us, length us, event | category | flops | bytes accessed | tf_op | source)
XLA Modules:
  0.0 56.7 jit_solution(3378384151355080758)
XLA Ops:
  0.0 55.9 %mixer.1 = bf16[512,512]{1,0:T(8,128)(2,1)S(1)} custom-call(bf16[512,1024]{1,0:T(8,128)(2,1)} %v_hbm.1, bf16[512,1024]{1,0:T(8,128)(2,1)} %g_hbm.1, bf16[512,128]{1,0:T(8,128)(2,1)} %k_hbm.1, bf16[512,128]{1,0:T(8,128)(2,1)} %q_hbm.1, f32[16,512]{1,0:T(8,128)} %log_hbm.1, f32[4,1024]{1,0:T(4,128)} %cv_hbm.1, f32[1,1024]{1,0:T(1,128)} %bitcast.5, ...), custom_call_target="tpu_custom_call" | custom-call | tf_op jit(solution)/shard_map/mixer/pallas_call | solution.py:655
  55.9 0.8 %copy.16 = bf16[512,512]{1,0:T(8,128)(2,1)} copy(bf16[512,512]{1,0:T(8,128)(2,1)S(1)} %mixer.1) | data formatting | bytes 1048576

commit v4 on v3

--- a/solution.py
+++ b/solution.py
@@ -319,10 +319,11 @@
 
     def rolled(window, lo, w_ref, b_ref, sl):
         x = xpad[window, lo : lo + LANES].astype(F32)
-        acc = b_ref[:, sl] + w_ref[3:4, sl] * x[PAD:]
+        w = 0.5 * w_ref[:, sl]
+        acc = 0.5 * b_ref[:, sl] + w[3:4] * x[PAD:]
         for back in range(1, 4):
-            acc = acc + w_ref[3 - back : 4 - back, sl] * pltpu.roll(x, back, axis=0)[PAD:]
-        return silu(acc).astype(BF16)
+            acc = acc + w[3 - back : 4 - back] * pltpu.roll(x, back, axis=0)[PAD:]
+        return (acc + acc * jnp.tanh(acc)).astype(BF16)
 
     def conv(c, top):
         at = pl.ds(pl.multiple_of(c * CH, CH), CH)
@@ -333,7 +334,6 @@
         keys_t[c] = kt
         if top:
             keys0[...] = keys
-        qs[at, :] = rolled(window, width + 128, cq_ref, bq_ref, one)
         for j in range(slabs):
             sl = slice(j * LANES, (j + 1) * LANES)
             v = rolled(window, j * LANES, cv_ref, bv_ref, sl)
@@ -355,7 +355,6 @@
         conv(chunks - i, False)
         return 0
 
-    lax.fori_loop(1, 3, conv_step, 0)
 
     pl.semaphore_wait(barrier, n_seq - 1 + 3)
     for halo in halos:
@@ -363,10 +362,7 @@
     for i in range(1, ROW):
         a_copy(i).start()
     ra[me] = abuf[...]
-    for k in range(4):
-        w_copy(k).start()
-
-    lax.fori_loop(3, chunks, conv_step, 0)
+    lax.fori_loop(1, chunks, conv_step, 0)
     conv(0, True)
     for q in range(slabs):
         sl = slice(q * LANES, (q + 1) * LANES)
@@ -388,9 +384,10 @@
         here = xpad[PAD : 2 * PAD, sl]
         return here, dot(shift_top[...], jnp.concatenate([above, here], axis=0))
 
-    x, moved = top_rows(slice(width, width + 256))
-    keys0[head, :] = taps(x[:, :128], moved[:, :128], PAD, ck_ref, bk_ref, slice(0, 128))
-    qs[head, :] = taps(x[:, 128:], moved[:, 128:], PAD, cq_ref, bq_ref, slice(0, 128))
+    x_top, moved_top = top_rows(slice(width, width + 256))
+    keys0[head, :] = taps(
+        x_top[:, :128], moved_top[:, :128], PAD, ck_ref, bk_ref, slice(0, 128)
+    )
     kt = keys0[...].astype(F32).T.astype(BF16)
     keys_t[0] = kt
     for j in range(width // 256):
@@ -415,6 +412,19 @@
 
     far_first(f_copy)
     rf[me] = fbuf[me]
+    for k in range(4):
+        w_copy(k).start()
+
+    def query(c, _):
+        at = pl.ds(pl.multiple_of(c * CH, CH), CH)
+        window = pl.ds(pl.multiple_of(c * CH, CH), CH + PAD)
+        qs[at, :] = rolled(window, width + 128, cq_ref, bq_ref, slice(0, 128))
+        return 0
+
+    lax.fori_loop(0, chunks, query, 0)
+    qs[head, :] = taps(
+        x_top[:, 128:], moved_top[:, 128:], PAD, cq_ref, bq_ref, slice(0, 128)
+    )
     for i in range(1, ROW):
         a_copy(i).wait_recv()
     for i in range(1, n_seq // ROW):

time: 56.8 us -> 55.7 us (0.981)
  Pallas kernels: 55.9 us -> 54.8 us
    pallas_call x1, Pallas kernels: 55.9 us -> 54.8 us  [shards(): pl.pallas_call(functools.partial(kernel, n_seq), out_shape=jax.ShapeDtype...]
where the time goes in v4:
time: 55.7 us; the launch traced here: 55.6 us
  Pallas kernels  54.8 us (98%)
  local copies, waits for them, and re-layouts  0.8 us (1%)
    pallas_call x1, Pallas kernels, shards(): pl.pallas_call(functools.partial(kernel, n_seq), out_shape=jax.ShapeDtype...  54.8 us

profile of v4, /device:TPU:1, one launch (start us, length us, event | category | flops | bytes accessed | tf_op | source)
XLA Modules:
  0.0 55.6 jit_solution(875666838555436969)
XLA Ops:
  0.0 54.8 %mixer.1 = bf16[512,512]{1,0:T(8,128)(2,1)S(1)} custom-call(bf16[512,1024]{1,0:T(8,128)(2,1)} %v_hbm.1, bf16[512,1024]{1,0:T(8,128)(2,1)} %g_hbm.1, bf16[512,128]{1,0:T(8,128)(2,1)} %k_hbm.1, bf16[512,128]{1,0:T(8,128)(2,1)} %q_hbm.1, f32[16,512]{1,0:T(8,128)} %log_hbm.1, f32[4,1024]{1,0:T(4,128)} %cv_hbm.1, f32[1,1024]{1,0:T(1,128)} %bitcast.5, ...), custom_call_target="tpu_custom_call" | custom-call | tf_op jit(solution)/shard_map/mixer/pallas_call | solution.py:665
  54.8 0.8 %copy.16 = bf16[512,512]{1,0:T(8,128)(2,1)} copy(bf16[512,512]{1,0:T(8,128)(2,1)S(1)} %mixer.1) | data formatting | bytes 1048576

commit v5 on v4

--- a/solution.py
+++ b/solution.py
@@ -15,6 +15,7 @@
 PAD = 16
 LANES = 128
 ROW = 8
+EARLY = 9
 
 
 def dot(a, b):
@@ -466,19 +467,29 @@
 
     lax.fori_loop(0, chunks, local, 0)
 
-    def await_f(i, _):
-        b = lax.rem(me + i, n_seq)
-        f_copy(b, b).wait_recv()
-        return 0
-
-    lax.fori_loop(1, n_seq, await_f, 0)
     for i in range(1, n_seq // ROW):
         b_copy(i).wait_recv()
     state = jnp.zeros((seg // 8, 8, LANES), F32)
     for b in range(n_seq):
+        @pl.when(me != b)
+        def _(b=b):
+            f_copy(b, b).wait_recv()
+
         sbuf[b] = state.astype(BF16).reshape(seg, LANES)
+        if b < EARLY:
+
+            @pl.when(me != b)
+            def _(b=b):
+                s_copy(b, me).start()
+
         state = ra[b, pl.ds(me // split, 1), :][None] * state + rf[b].astype(F32).reshape(seg // 8, 8, LANES)
-    far_first(s_copy)
+    for dy, dz in hops:
+        at = lax.rem(row + dy, n_seq // ROW) * ROW + lax.rem(col + dz, ROW)
+
+        @pl.when(at >= EARLY)
+        def _(at=at):
+            s_copy(at, me).start()
+
     s_in[me] = sbuf[me]
 
     gate_load.wait()
@@ -585,15 +596,6 @@
             h_copy(m, way).wait_recv()
             c_send[m, way] = (join[m, way] + h_recv[m, way].astype(F32)).astype(BF16)
             c_copy(m, way).start()
-    for m in range(2):
-        for way in range(2):
-            d_copy(m, 1 - way).wait_recv()
-            c_copy(m, way).wait_recv()
-            lo = way * quarter
-            total = own[m, lo : lo + quarter, :]
-            total = total + d_recv[m, 1 - way].astype(F32) + c_recv[m, way].astype(F32)
-            out_ref[m * half + lo : m * half + lo + quarter, :] = total.astype(BF16)
-
     for halo in halos:
         halo.wait_send()
 
@@ -612,6 +614,15 @@
         w_copy(k).wait_send()
     for p in range(2, 4):
         y_copy(p).wait_send()
+    for m in range(2):
+        for way in range(2):
+            d_copy(m, 1 - way).wait_recv()
+            c_copy(m, way).wait_recv()
+            lo = way * quarter
+            total = own[m, lo : lo + quarter, :]
+            total = total + d_recv[m, 1 - way].astype(F32) + c_recv[m, way].astype(F32)
+            out_ref[m * half + lo : m * half + lo + quarter, :] = total.astype(BF16)
+
     for m in range(2):
         for way in range(2):
             h_copy(m, way).wait_send()

time: 55.7 us -> 53.2 us (0.955)
  Pallas kernels: 54.8 us -> 52.2 us
    pallas_call x1, Pallas kernels: 54.8 us -> 52.2 us  [shards(): pl.pallas_call(functools.partial(kernel, n_seq), out_shape=jax.ShapeDtype...]
where the time goes in v5:
time: 53.2 us; the launch traced here: 53 us
  Pallas kernels  52.2 us (98%)
  local copies, waits for them, and re-layouts  0.8 us (2%)
    pallas_call x1, Pallas kernels, shards(): pl.pallas_call(functools.partial(kernel, n_seq), out_shape=jax.ShapeDtype...  52.2 us

profile of v5, /device:TPU:1, one launch (start us, length us, event | category | flops | bytes accessed | tf_op | source)
XLA Modules:
  0.0 53.0 jit_solution(13193903306238621416)
XLA Ops:
  0.0 52.2 %mixer.1 = bf16[512,512]{1,0:T(8,128)(2,1)S(1)} custom-call(bf16[512,1024]{1,0:T(8,128)(2,1)} %v_hbm.1, bf16[512,1024]{1,0:T(8,128)(2,1)} %g_hbm.1, bf16[512,128]{1,0:T(8,128)(2,1)} %k_hbm.1, bf16[512,128]{1,0:T(8,128)(2,1)} %q_hbm.1, f32[16,512]{1,0:T(8,128)} %log_hbm.1, f32[4,1024]{1,0:T(4,128)} %cv_hbm.1, f32[1,1024]{1,0:T(1,128)} %bitcast.5, ...), custom_call_target="tpu_custom_call" | custom-call | tf_op jit(solution)/shard_map/mixer/pallas_call | solution.py:676
  52.2 0.8 %copy.16 = bf16[512,512]{1,0:T(8,128)(2,1)} copy(bf16[512,512]{1,0:T(8,128)(2,1)S(1)} %mixer.1) | data formatting | bytes 1048576
